TPU v7x, 128 devices: a whole 4x4x4 slice. The times are simulated.
128 devices in a mesh: group: 8 (over x_lo, y), tp: 16 (over z, x_hi, core).
Axes of the slice: x: 4 (x_hi: 2, x_lo: 2; x = x_hi * 2 + x_lo), y: 4, z: 4, core: 2. Of those that a mesh axis runs over, the one named last changes fastest.
Arguments:
- weight_tiles: bfloat16 [8, 1792, 128, 128], P('group', 'tp'), may hold values from -0.0625 to 0.0625
- gradients: bfloat16 [8, 1792, 128, 128], P('group', 'tp'), may hold values from -6 to 6
- momentum: float32 [8, 1792, 128, 128], P('group', 'tp'), may hold values from -6 to 6
- slot_place: int32 [1792], replicated, may hold values from 0 to 111, as said below
- refresh: int32 [2], replicated, may hold values from 0 to 7, as said below
Outputs:
- slices: bfloat16 [8, 2, 2, 2048, 7168], P('group', None, None, 'tp')
- block_scales: bfloat16 [8, 2, 2, 16, 56], P('group', None, None, 'tp')
Inputs may be any that keep to these rules, and one draw needn't show every extreme that they name: `slot_place`: for each tensor slice r, the slots s with (s mod (112)) // 7 == r hold every position 0 to 111 once. `refresh`: distinct expert ids.
All inputs are finite; a program needn't handle non-finite values.
Results may differ from a plain program's by a relative error of at most 0.009.
Values may be sent and summed in bfloat16 or wider, within the bound.
No kernel may reach another device: no remote copies, remote signals or barrier semaphores. Data moves between devices by JAX's collectives and lax.ppermute only.
A program may use at most 128 MiB of HBM per device.

v0:
```python
import jax
import jax.numpy as jnp
from jax import lax
from jax.sharding import PartitionSpec as P

D = 7168


learn_rate = 0.01
decay_rate = 0.1
momentum_decay = 0.9
epsilon = 1e-06
fp_range = 448.0


def spread(x, axis, root):
    mine = lax.axis_index(axis) == root
    return lax.psum(jnp.where(mine, x, jnp.zeros_like(x)), axis)


def updated_blocks(weight_tiles, gradients, momentum):
    updated = weight_tiles.astype(jnp.float32) * (1.0 - learn_rate * decay_rate) - learn_rate * (
        momentum_decay * momentum + gradients.astype(jnp.float32)
    )
    largest = jnp.max(jnp.abs(updated), axis=(2, 3))
    scales = ((largest + epsilon) / fp_range).astype(jnp.bfloat16)
    payload = (updated / scales.astype(jnp.float32)[:, :, None, None]).astype(jnp.bfloat16)
    return (payload, scales)


def arrange(payload, scales, positions):
    count = payload.shape[0]
    tile = payload.shape[2]
    columns = D // tile
    row_blocks = payload.shape[1] // columns
    ordering = jnp.argsort(positions)
    placed = jnp.take(payload, ordering, axis=1)
    placed = placed.reshape(count, row_blocks, columns, tile, tile).transpose(0, 1, 3, 2, 4)
    placed = placed.reshape(count, 2, row_blocks * tile // 2, columns * tile)
    scaled = jnp.take(scales, ordering, axis=1).reshape(count, 2, row_blocks // 2, columns)
    return (placed, scaled)


def local(weight_tiles, gradients, momentum, slot_place, refresh):
    owners = lax.axis_size("tp")
    slice_rank = lax.axis_index("tp")
    local_count = weight_tiles.shape[0]
    held = weight_tiles.shape[1]
    tile = weight_tiles.shape[2]
    per_slice = held // owners
    grid = slot_place.reshape(owners, owners, per_slice)
    mine = lax.dynamic_index_in_dim(grid, slice_rank, 1, keepdims=False).reshape(-1)
    payload, scales = updated_blocks(weight_tiles, gradients, momentum)
    local_blocks = payload.reshape(local_count, owners, per_slice, tile, tile)
    local_scales = scales.reshape(local_count, owners, per_slice)
    blocks = lax.all_to_all(local_blocks, "tp", split_axis=1, concat_axis=1, tiled=True)
    placing_scaled = lax.all_to_all(local_scales, "tp", split_axis=1, concat_axis=1, tiled=True)
    count = blocks.shape[0]
    placed, placed_scales = arrange(
        blocks.reshape(count, held, tile, tile), placing_scaled.reshape(count, held), mine
    )
    chosen_slices = []
    chosen_scales = []
    for which in range(refresh.shape[0]):
        chosen = refresh[which]
        root = chosen // local_count
        within = chosen % local_count
        piece = lax.dynamic_index_in_dim(placed, within, 0, keepdims=False)
        scaled = lax.dynamic_index_in_dim(placed_scales, within, 0, keepdims=False)
        piece, scaled = (spread(piece, "group", root), spread(scaled, "group", root))
        chosen_slices.append(piece)
        chosen_scales.append(scaled)
    slices = jnp.stack(chosen_slices)
    block_scales = jnp.stack(chosen_scales)
    return (slices[None], block_scales[None])


def solution(mesh):
    placed = (
        P("group", "tp", None, None),
        P("group", "tp", None, None),
        P("group", "tp", None, None),
        P(),
        P(),
    )
    return jax.shard_map(
        local,
        mesh=mesh,
        in_specs=placed,
        out_specs=(P("group", None, None, "tp", None), P("group", None, None, "tp", None)),
        check_vma=False,
    )
```

profile of v0, /device:TPU:1, one launch (start us, length us, event | category | flops | bytes accessed | tf_op | source)
XLA Modules:
  0.0 294.2 jit_solution(14274418370934694640)
XLA Ops:
  7.2 8.5 %abs_reduce_fusion = f32[112]{0:T(128)S(1)} fusion(bf16[1,112,128,128]{3,2,1,0:T(8,128)(2,1)} %param.6, f32[1,112,128,128]{3,2,1,0:T(8,128)} %param.7, bf16[1,112,128,128]{3,2,1,0:T(8,128)(2,1)} %param.5), kind=kLoop, calls=%fused_computation.4 | loop fusion | flops 16514960 | bytes 14680512 | tf_op jit(solution)/shard_map/reduce_max | solution.py:25
  15.7 0.7 convert_element_type.44
  16.4 9.3 %all-to-all-start.1 = ((bf16[1,16,7]{2,0,1:T(2,128)(2,1)}), bf16[1,16,7]{2,0,1:T(2,128)(2,1)S(1)}, u32[]{:S(2)}, u32[]{:S(2)}) async-start(bf16[1,16,7]{2,0,1:T(2,128)(2,1)} %convert_element_type.44), calls=%async_computation.1 | async-start | bytes 16384 | tf_op jit(solution)/shard_map/all_to_all | solution.py:57
  25.7 7.9 %divide_convert_fusion = bf16[1,112,128,128]{3,2,1,0:T(8,128)(2,1)} fusion(f32[112]{0:T(128)S(1)} %get-tuple-element.21, bf16[1,112,128,128]{3,2,1,0:T(8,128)(2,1)} %param.6, f32[1,112,128,128]{3,2,1,0:T(8,128)} %param.7, bf16[1,112,128,128]{3,2,1,0:T(8,128)(2,1)} %param.5), kind=kLoop, calls=%fused_computation.3 | loop fusion | flops 16515072 | bytes 18350528 | tf_op jit(solution)/shard_map/convert_element_type | solution.py:27
  33.6 0.0 copy-start.1
  33.6 0.0 copy-start
  33.6 0.0 all-to-all-done.1
  33.6 7.4 %all-to-all-start = ((bf16[1,16,7,128,128]{4,3,2,0,1:T(8,128)(2,1)}), bf16[1,16,7,128,128]{4,3,2,0,1:T(8,128)(2,1)}, u32[]{:S(2)}, u32[]{:S(2)}) async-start(bf16[1,16,7,128,128]{4,3,2,0,1:T(8,128)(2,1)} %bitcast.20), calls=%async_computation | async-start | bytes 7340032 | tf_op jit(solution)/shard_map/all_to_all | solution.py:56
  40.9 0.0 all-reduce.4.cloned.1.call-start
  41.0 0.0 copy-done.1
  41.0 0.6 fusion.1
  42.8 0.0 copy-done
  42.8 0.2 reshape.136
  43.1 0.1 reshape.137
  43.1 2.5 sort.17
  45.7 0.1 reshape.153
  45.8 1.2 gather_fusion.1
  47.1 0.1 broadcast_in_dim.31
  47.2 39.1 %all-to-all-done = bf16[1,16,7,128,128]{4,3,2,0,1:T(8,128)(2,1)} async-done(((bf16[1,16,7,128,128]{4,3,2,0,1:T(8,128)(2,1)}), bf16[1,16,7,128,128]{4,3,2,0,1:T(8,128)(2,1)}, u32[]{:S(2)}, u32[]{:S(2)}) %all-to-all-start) | async-done | bytes 3670048 | tf_op jit(solution)/shard_map/all_to_all | solution.py:56
  86.2 4.9 %gather_fusion = bf16[112,128,128]{2,1,0:T(8,128)(2,1)} fusion(bf16[112,128,128]{2,1,0:T(8,128)(2,1)} %bitcast.2, s32[1024]{0:T(1024)S(1)} %pad_clamp_fusion), kind=kCustom, calls=%fused_computation | custom fusion | bytes 7340480 | tf_op jit(solution)/shard_map/jit(_take)/gather | solution.py:37
  91.2 5.0 %select_bitcast_fusion.1 = (bf16[1,2,128,56,128]{4,2,3,1,0:T(8,128)(2,1)}, bf16[1,2,128,56,128]{4,2,3,1,0:T(8,128)(2,1)}) fusion(pred[]{:T(512)S(6)} %eq.11, bf16[1,2,56,128,128]{4,3,2,1,0:T(8,128)(2,1)} %bitcast.19, pred[2,56]{1,0:T(4,128)(4,1)S(1)} %broadcast_in_dim.31, pred[]{:T(512)S(6)} %eq.12), kind=kLoop, calls=%fused_computation.7 | loop fusion | flops 5505024 | bytes 11010162 | tf_op jit(solution)/shard_map/jit(_where)/select_n | solution.py:18
  96.1 6.0 %copy.13 = bf16[1,2,128,56,128]{2,4,3,1,0:T(8,128)(2,1)} copy(bf16[1,2,128,56,128]{4,2,3,1,0:T(8,128)(2,1)} %get-tuple-element.18) | data formatting | bytes 7340032 | tf_op jit(solution)/shard_map/jit(_where)/select_n | solution.py:18
  102.1 5.9 %copy.14 = bf16[1,2,128,56,128]{2,4,3,1,0:T(8,128)(2,1)} copy(bf16[1,2,128,56,128]{4,2,3,1,0:T(8,128)(2,1)} %get-tuple-element.19) | data formatting | bytes 7340032 | tf_op jit(solution)/shard_map/jit(_where)/select_n | solution.py:18
  108.0 0.0 all-reduce.4.cloned.1.call-update
  108.1 0.1 stack.21
  108.2 0.1 stack.22
  108.2 16.5 %all-reduce = (bf16[1,2,1,56]{3,1,2,0:T(2,128)(2,1)S(1)}, bf16[1,2,1,56]{3,1,2,0:T(2,128)(2,1)S(1)}) all-reduce(bf16[1,2,1,56]{3,1,2,0:T(2,128)(2,1)S(1)} %stack.22, bf16[1,2,1,56]{3,1,2,0:T(2,128)(2,1)S(1)} %stack.21), channel_id=1, replica_groups=mesh['group'=8,'tp'=16] {'group'}, use_global_device_ids=true, to_apply=%region_5.6 | all-reduce | flops 224 | bytes 896 | tf_op jit(solution)/shard_map/psum | solution.py:18
  124.7 0.6 maximum_bitcast_fusion.1
  125.3 145.4 %all-reduce.4.cloned.1.call-done = (bf16[1,2,128,7168]{2,3,1,0:T(8,128)(2,1)}, bf16[1,2,128,7168]{2,3,1,0:T(8,128)(2,1)}) async-done(((bf16[1,2,128,7168]{2,3,1,0:T(8,128)(2,1)}, bf16[1,2,128,7168]{2,3,1,0:T(8,128)(2,1)}), (bf16[1,2,128,7168]{2,3,1,0:T(8,128)(2,1)}, bf16[1,2,128,7168]{2,3,1,0:T(8,128)(2,1)})) %all-reduce.4.cloned.1.call-update) | async-done | bytes 7340048 | tf_op jit(solution)/shard_map/psum | solution.py:18
  270.7 6.8 %maximum_bitcast_fusion = bf16[1,2,2,128,7168]{3,4,2,1,0:T(8,128)(2,1)} fusion(bf16[1,2,128,7168]{2,3,1,0:T(8,128)(2,1)} %get-tuple-element.14, bf16[1,2,128,7168]{2,3,1,0:T(8,128)(2,1)} %get-tuple-element.15), kind=kLoop, calls=%fused_computation.2 | loop fusion | flops 3670016 | bytes 14680064 | tf_op jit(solution)/shard_map/broadcast_in_dim | solution.py:75
  277.5 9.9 %copy.16 = bf16[1,2,2,128,7168]{4,3,2,1,0:T(8,128)(2,1)} copy(bf16[1,2,2,128,7168]{3,4,2,1,0:T(8,128)(2,1)} %maximum_bitcast_fusion) | data formatting | bytes 14680064
  (8 shorter events, 0.1 us)
Async XLA Ops:
  16.4 17.2 %all-to-all-start.1 = ((bf16[1,16,7]{2,0,1:T(2,128)(2,1)}), bf16[1,16,7]{2,0,1:T(2,128)(2,1)S(1)}, u32[]{:S(2)}, u32[]{:S(2)}) async-start(bf16[1,16,7]{2,0,1:T(2,128)(2,1)} %convert_element_type.44), calls=%async_computation.1 | async-start | bytes 16384 | tf_op jit(solution)/shard_map/all_to_all | solution.py:57
  33.6 7.4 %copy-start.1 = (s32[2]{0:T(128)S(1)}, s32[2]{0:T(128)}, u32[]{:S(2)}) copy-start(s32[2]{0:T(128)} %param.9) | copy-start | bytes 28
  33.6 9.2 %copy-start = (s32[1792]{0:T(1024)S(1)}, s32[1792]{0:T(1024)}, u32[]{:S(2)}) copy-start(s32[1792]{0:T(1024)} %param.8) | copy-start | bytes 21508
  33.6 52.7 %all-to-all-start = ((bf16[1,16,7,128,128]{4,3,2,0,1:T(8,128)(2,1)}), bf16[1,16,7,128,128]{4,3,2,0,1:T(8,128)(2,1)}, u32[]{:S(2)}, u32[]{:S(2)}) async-start(bf16[1,16,7,128,128]{4,3,2,0,1:T(8,128)(2,1)} %bitcast.20), calls=%async_computation | async-start | bytes 7340032 | tf_op jit(solution)/shard_map/all_to_all | solution.py:56
  40.9 229.7 %all-reduce.4.cloned.1.call-start = ((), (), s32[]{:S(2)}) async-start(), calls=%async_computation.2 | async-start | bytes 14680064 | tf_op jit(solution)/shard_map/psum | solution.py:18
Sparse Core Ops, SparseCore 0:
  108.2 162.4 all-reduce.3
where the time goes:
time: 295 us; the launch traced here: 294 us
  waiting for transfers between devices  184 us (62%)
  other arithmetic  31.3 us (11%)
  local copies, waits for them, and re-layouts  30 us (10%)
  starting transfers between devices  16.7 us (6%)
  blocking collectives  16.5 us (6%)
  between operations  15.3 us (5%)
    psum x1, waiting for transfers between devices, spread(): return lax.psum(jnp.where(mine, x, jnp.zeros_like(x)), axis)  145 us
    all_to_all x1, waiting for transfers between devices, local(): lax.all_to_all(local_blocks, 'tp', split_axis=1, concat_axis=1, tiled=True)  39.1 us
    psum x1, blocking collectives, spread(): return lax.psum(jnp.where(mine, x, jnp.zeros_like(x)), axis)  16.5 us
    select_n x2, local copies, waits for them, and re-layouts, spread(): return lax.psum(jnp.where(mine, x, jnp.zeros_like(x)), axis)  11.9 us
    unnamed x5, local copies, waits for them, and re-layouts  9.94 us
    all_to_all x1, starting transfers between devices, local(): lax.all_to_all(local_scales, 'tp', split_axis=1, concat_axis=1, tiled=True)  9.28 us
    reduce_max x1, other arithmetic, updated_blocks(): largest = jnp.max(jnp.abs(updated), axis=(2, 3))  8.54 us
    convert_element_type x1, other arithmetic, updated_blocks(): (updated / scales.astype(jnp.float32)[:, :, None, None]).astype(jnp.bfloa...  7.87 us
  transfers between devices with their start and end apart: 3, of which 2 were waited for; matrix products, arithmetic and copies ran while one was open for 5% of the time, Pallas kernels for 0%

commit v1 on v0

v1 whole, which is shorter than its diff:
```python
import functools

import jax
import jax.numpy as jnp
from jax import lax
from jax.experimental import pallas as pl
from jax.experimental.pallas import tpu as pltpu
from jax.sharding import PartitionSpec as P

D = 7168
TILE = 128
COLUMNS = D // TILE
SLOT_K = 7
N_GROUP = 8
N_TP = 16
BAND = TILE // N_GROUP
SCALE_ROWS = 8
ROWS = SLOT_K * BAND + SCALE_ROWS
PART = COLUMNS // 2 * TILE

learn_rate = 0.01
decay_rate = 0.1
momentum_decay = 0.9
epsilon = 1e-06
fp_range = 448.0

VMEM_LIMIT = 60 << 20


def step_kernel(w_ref, g_ref, m_ref, out_ref):
    for r in range(out_ref.shape[1]):
        tiles = pl.ds(r * SLOT_K, SLOT_K)
        updated = w_ref[tiles].astype(jnp.float32) * (1.0 - learn_rate * decay_rate) - learn_rate * (
            momentum_decay * m_ref[tiles] + g_ref[tiles].astype(jnp.float32)
        )
        largest = jnp.max(jnp.max(jnp.abs(updated), axis=1, keepdims=True), axis=2, keepdims=True)
        scale = ((largest + epsilon) / fp_range).astype(jnp.bfloat16)
        payload = (updated * (1.0 / scale.astype(jnp.float32))).astype(jnp.bfloat16)
        for k in range(SLOT_K):
            out_ref[:, r, k * BAND : (k + 1) * BAND, :] = payload[k].reshape(N_GROUP, BAND, TILE)
        row = lax.broadcasted_iota(jnp.int32, (SCALE_ROWS, TILE), 0)
        rows = jnp.zeros((SCALE_ROWS, TILE), jnp.float32)
        for k in range(SLOT_K):
            rows = jnp.where(row == k, jnp.broadcast_to(scale[k].astype(jnp.float32), rows.shape), rows)
        rows = rows.astype(jnp.bfloat16)
        for g in range(N_GROUP):
            out_ref[g, r, SLOT_K * BAND :, :] = rows


def step(weight_tiles, gradients, momentum, slices=2):
    tiles = slices * SLOT_K
    spec = pl.BlockSpec((tiles, TILE, TILE), lambda i: (i, 0, 0))
    return pl.pallas_call(
        step_kernel,
        grid=(N_TP // slices,),
        in_specs=[spec] * 3,
        out_specs=pl.BlockSpec((N_GROUP, slices, ROWS, TILE), lambda i: (0, i, 0, 0)),
        out_shape=jax.ShapeDtypeStruct((N_GROUP, N_TP, ROWS, TILE), jnp.bfloat16),
        compiler_params=pltpu.CompilerParams(vmem_limit_bytes=VMEM_LIMIT),
        name="step",
    )(weight_tiles, gradients, momentum)


def place_kernel(place_ref, refresh_ref, rank_ref, recv_ref, a_ref, b_ref, buf, placed, sem_in, sem_out):
    rank = rank_ref[0]
    fetch = [
        pltpu.make_async_copy(recv_ref.at[refresh_ref[j]], buf.at[j], sem_in.at[j])
        for j in range(2)
    ]
    for copy in fetch:
        copy.start()
    store = []
    for j in range(2):
        fetch[j].wait()

        def owner(t, _, j=j):
            for k in range(SLOT_K):
                p = place_ref[t * (N_TP * SLOT_K) + rank * SLOT_K + k]
                half = (p >= COLUMNS).astype(jnp.int32)
                column = pl.multiple_of((p - COLUMNS * half) * TILE, TILE)
                placed[j, half, :, pl.ds(column, TILE)] = buf[j, t, k * BAND : (k + 1) * BAND, :]
            return 0

        lax.fori_loop(0, N_TP, owner, 0)
        for side, ref in enumerate((a_ref, b_ref)):
            copy = pltpu.make_async_copy(
                placed.at[j, :, :, pl.ds(side * PART, PART)], ref.at[j], sem_out.at[j, side]
            )
            copy.start()
            store.append(copy)
    for copy in store:
        copy.wait()


def place(slot_place, refresh, rank, recv):
    part = jax.ShapeDtypeStruct((2, 2, BAND, PART), jnp.bfloat16)
    smem = pl.BlockSpec(memory_space=pltpu.SMEM)
    return pl.pallas_call(
        place_kernel,
        in_specs=[smem, smem, smem, pl.BlockSpec(memory_space=pl.ANY)],
        out_specs=[pl.BlockSpec(memory_space=pl.ANY)] * 2,
        out_shape=[part, part],
        scratch_shapes=[
            pltpu.VMEM((2, N_TP, ROWS, TILE), jnp.bfloat16),
            pltpu.VMEM((2, 2, BAND, D), jnp.bfloat16),
            pltpu.SemaphoreType.DMA((2,)),
            pltpu.SemaphoreType.DMA((2, 2)),
        ],
        compiler_params=pltpu.CompilerParams(vmem_limit_bytes=VMEM_LIMIT),
        name="place",
    )(slot_place, refresh, rank, recv)


def scales_kernel(place_ref, refresh_ref, rank_ref, recv_ref, out_ref, buf, sem):
    rank = rank_ref[0]
    fetch = [
        pltpu.make_async_copy(
            recv_ref.at[refresh_ref[j], :, pl.ds(SLOT_K * BAND, SCALE_ROWS), :], buf.at[j], sem.at[j]
        )
        for j in range(2)
    ]
    for copy in fetch:
        copy.start()
    at = lax.broadcasted_iota(jnp.int32, (SCALE_ROWS, TILE), 0) * TILE + lax.broadcasted_iota(
        jnp.int32, (SCALE_ROWS, TILE), 1
    )
    for j in range(2):
        fetch[j].wait()

        def owner(t, halves, j=j):
            rows = buf[j, t].astype(jnp.float32)
            first, second = halves
            for k in range(SLOT_K):
                p = place_ref[t * (N_TP * SLOT_K) + rank * SLOT_K + k]
                first = jnp.where(at == k * TILE + p, rows, first)
                second = jnp.where(at == k * TILE + p - COLUMNS, rows, second)
            return first, second

        empty = jnp.zeros((SCALE_ROWS, TILE), jnp.float32)
        for half, found in enumerate(lax.fori_loop(0, N_TP, owner, (empty, empty))):
            total = jnp.sum(found, axis=0, keepdims=True)
            out_ref[j, half] = total[:, :COLUMNS].astype(jnp.bfloat16)


def scales(slot_place, refresh, rank, recv):
    smem = pl.BlockSpec(memory_space=pltpu.SMEM)
    return pl.pallas_call(
        scales_kernel,
        in_specs=[smem, smem, smem, pl.BlockSpec(memory_space=pl.ANY)],
        out_specs=pl.BlockSpec(memory_space=pltpu.VMEM),
        out_shape=jax.ShapeDtypeStruct((2, 2, 1, COLUMNS), jnp.bfloat16),
        scratch_shapes=[
            pltpu.VMEM((2, N_TP, SCALE_ROWS, TILE), jnp.bfloat16),
            pltpu.SemaphoreType.DMA((2,)),
        ],
        name="scales",
    )(slot_place, refresh, rank, recv)


def join_kernel(n, bands_ref, *refs):
    pieces, out_ref, buf, sem_in, sem_out = refs[: 2 * n], refs[2 * n], refs[2 * n + 1], refs[2 * n + 2], refs[2 * n + 3]
    fetch = [pltpu.make_async_copy(piece, buf.at[i], sem_in.at[i]) for i, piece in enumerate(pieces)]
    for copy in fetch:
        copy.start()
    store = []
    for i in range(2 * n):
        fetch[i].wait()
        row = pl.multiple_of(bands_ref[i // 2] * BAND, BAND)
        copy = pltpu.make_async_copy(
            buf.at[i], out_ref.at[:, :, pl.ds(row, BAND), pl.ds((i % 2) * PART, PART)], sem_out.at[i]
        )
        copy.start()
        store.append(copy)
    for copy in store:
        copy.wait()


def join(bands, pieces):
    n = len(pieces) // 2
    return pl.pallas_call(
        functools.partial(join_kernel, n),
        in_specs=[pl.BlockSpec(memory_space=pltpu.SMEM)] + [pl.BlockSpec(memory_space=pl.ANY)] * (2 * n),
        out_specs=pl.BlockSpec(memory_space=pl.ANY),
        out_shape=jax.ShapeDtypeStruct((2, 2, TILE, D), jnp.bfloat16),
        scratch_shapes=[
            pltpu.VMEM((2 * n, 2, 2, BAND, PART), jnp.bfloat16),
            pltpu.SemaphoreType.DMA((2 * n,)),
            pltpu.SemaphoreType.DMA((2 * n,)),
        ],
        compiler_params=pltpu.CompilerParams(vmem_limit_bytes=VMEM_LIMIT),
        name="join",
    )(bands, *pieces)


def moves(to):
    return [(4 * x + y, 4 * to(x, y)[0] + to(x, y)[1]) for x in range(2) for y in range(4)]


UP = moves(lambda x, y: (x, (y + 1) % 4))
DOWN = moves(lambda x, y: (x, (y + 3) % 4))
ACROSS = moves(lambda x, y: (1 - x, y))


def gather(a, b):
    up, down, across = (functools.partial(lax.ppermute, axis_name="group", perm=perm) for perm in (UP, DOWN, ACROSS))
    xb = across(b)
    a_prev, a_next = up(a), down(a)
    xa = across(a)
    a_far = up(a_prev)
    b_prev, b_next = up(b), down(b)
    xa_prev = across(a_prev)
    xb_prev, xb_next = up(xb), down(xb)
    xa_next = across(a_next)
    b_far = up(b_prev)
    xb_far = down(xb_next)
    xa_far = across(a_far)
    return [a, b, a_prev, b_prev, a_next, b_next, a_far, b_far, xa, xb, xa_prev, xb_prev, xa_next, xb_next, xa_far, xb_far]


def local(weight_tiles, gradients, momentum, slot_place, refresh):
    group = lax.axis_index("group")
    rank = lax.axis_index("tp").astype(jnp.int32).reshape(1)
    cut = step(weight_tiles[0], gradients[0], momentum[0])
    recv = lax.all_to_all(cut.reshape(N_GROUP * N_TP, ROWS, TILE), ("group", "tp"), 0, 0, tiled=True)
    recv = recv.reshape(N_GROUP, N_TP, ROWS, TILE)
    a, b = place(slot_place, refresh, rank, recv)
    block_scales = scales(slot_place, refresh, rank, recv)
    x, y = group // 4, group % 4
    ys = jnp.stack([y, (y + 3) % 4, (y + 1) % 4, (y + 2) % 4])
    bands = jnp.concatenate([4 * x + ys, 4 * (1 - x) + ys]).astype(jnp.int32)
    slices = join(bands, gather(a, b))
    return (slices[None], block_scales[None])


def solution(mesh):
    placed = (
        P("group", "tp", None, None),
        P("group", "tp", None, None),
        P("group", "tp", None, None),
        P(),
        P(),
    )
    return jax.shard_map(
        local,
        mesh=mesh,
        in_specs=placed,
        out_specs=(P("group", None, None, "tp", None), P("group", None, None, "tp", None)),
        check_vma=False,
    )
```

time: 295 us -> 137 us (0.46)
  waiting for transfers between devices: 184 us -> 87.6 us
  other arithmetic: 31.3 us -> 0.66 us
  local copies, waits for them, and re-layouts: 30 us -> 1.27 us
  Pallas kernels: 0 us -> 22.7 us
  blocking collectives: 16.5 us -> 0 us
  between operations: 15.3 us -> 0.73 us
  starting transfers between devices: 16.7 us -> 21.9 us
    psum x1 -> x0, waiting for transfers between devices: 145 us -> none  [spread(): return lax.psum(jnp.where(mine, x, jnp.zeros_like(x)), axis)]
    ppermute x0 -> x14, waiting for transfers between devices: none -> 37.8 us  [the longest x1 9.83 us: gather(): b_far = up(b_prev)]
    pallas_call x0 -> x4, Pallas kernels: none -> 22.7 us  [the longest x1 9.93 us: step(): pl.pallas_call(step_kernel, grid=(N_TP // slices,), in_specs=[spec] * 3,...]
    psum x1 -> x0, blocking collectives: 16.5 us -> none  [spread(): return lax.psum(jnp.where(mine, x, jnp.zeros_like(x)), axis)]
    select_n x2 -> x0, local copies, waits for them, and re-layouts: 11.9 us -> none  [spread(): return lax.psum(jnp.where(mine, x, jnp.zeros_like(x)), axis)]
    all_to_all x2 -> x1, waiting for transfers between devices: 39.1 us -> 49.8 us  [local(): lax.all_to_all(cut.reshape(N_GROUP * N_TP, ROWS, TILE), ('group', 'tp'),...]
    ppermute x0 -> x14, starting transfers between devices: none -> 9.97 us  [the longest x1 1.91 us: gather(): xa_far = across(a_far)]
    unnamed x5 -> x15, local copies, waits for them, and re-layouts: 9.94 us -> 1.27 us
  transfers between devices with their start and end apart: 3 -> 15, of which waited for: 2 -> 10; matrix products, arithmetic and copies ran while one was open for 5% -> 1% of each run, Pallas kernels for 0% -> 2%
where the time goes in v1:
time: 137 us; the launch traced here: 135 us
  waiting for transfers between devices  87.6 us (64%)
  Pallas kernels  22.7 us (17%)
  starting transfers between devices  21.9 us (16%)
    all_to_all x1, waiting for transfers between devices, local(): lax.all_to_all(cut.reshape(N_GROUP * N_TP, ROWS, TILE), ('group', 'tp'),...  49.8 us
    all_to_all x1, starting transfers between devices, local(): lax.all_to_all(cut.reshape(N_GROUP * N_TP, ROWS, TILE), ('group', 'tp'),...  11.9 us
    pallas_call x1, Pallas kernels, step(): pl.pallas_call(step_kernel, grid=(N_TP // slices,), in_specs=[spec] * 3,...  9.93 us
    ppermute x1, waiting for transfers between devices, gather(): b_far = up(b_prev)  9.83 us
    ppermute x1, waiting for transfers between devices, gather(): xb = across(b)  7.75 us
    ppermute x1, waiting for transfers between devices, gather(): xa = across(a)  7.43 us
    ppermute x1, waiting for transfers between devices, gather(): xa_next = across(a_next)  7.28 us
    pallas_call x1, Pallas kernels, join(): pl.pallas_call(functools.partial(join_kernel, n), in_specs=[pl.BlockSpec(...  6.61 us
  transfers between devices with their start and end apart: 15, of which 10 were waited for; matrix products, arithmetic and copies ran while one was open for 1% of the time, Pallas kernels for 2%

profile of v1, /device:TPU:1, one launch (start us, length us, event | category | flops | bytes accessed | tf_op | source)
XLA Modules:
  0.0 134.9 jit_solution(6068126958037911223)
XLA Ops:
  0.6 9.9 %step.1 = bf16[8,16,120,128]{3,2,1,0:T(8,128)(2,1)} custom-call(bf16[112,128,128]{2,1,0:T(8,128)(2,1)} %bitcast.19, bf16[112,128,128]{2,1,0:T(8,128)(2,1)} %bitcast.20, f32[112,128,128]{2,1,0:T(8,128)} %bitcast.17), custom_call_target="tpu_custom_call" | custom-call | tf_op jit(solution)/shard_map/step/pallas_call | solution.py:53
  10.6 11.9 %all-to-all-start = ((bf16[128,120,128]{2,1,0:T(8,128)(2,1)}), bf16[128,120,128]{2,1,0:T(8,128)(2,1)}, u32[]{:S(2)}, u32[]{:S(2)}) async-start(bf16[128,120,128]{2,1,0:T(8,128)(2,1)} %bitcast.16), calls=%async_computation | async-start | bytes 7864320 | tf_op jit(solution)/shard_map/all_to_all | solution.py:224
  22.5 49.8 %all-to-all-done = bf16[128,120,128]{2,1,0:T(8,128)(2,1)} async-done(((bf16[128,120,128]{2,1,0:T(8,128)(2,1)}), bf16[128,120,128]{2,1,0:T(8,128)(2,1)}, u32[]{:S(2)}, u32[]{:S(2)}) %all-to-all-start) | async-done | bytes 3932192 | tf_op jit(solution)/shard_map/all_to_all | solution.py:224
  72.3 3.6 %place.1 = (bf16[2,2,16,3584]{3,2,1,0:T(8,128)(2,1)}, bf16[2,2,16,3584]{3,2,1,0:T(8,128)(2,1)}) custom-call(s32[1792]{0:T(1024)} %place_ref.3, s32[2]{0:T(128)} %refresh_ref.3, s32[1]{0:T(128)} %bitcast.4.rank_ref, bf16[8,16,120,128]{3,2,1,0:T(8,128)(2,1)} %bitcast.9.recv_ref), custom_call_target="tpu_custom_call" | custom-call | tf_op jit(solution)/shard_map/place/pallas_call | solution.py:98
  75.9 0.9 collective-permute-start.6
  76.8 0.0 collective-permute-start.2
  76.8 1.5 %collective-permute-start = (bf16[2,2,16,3584]{3,2,1,0:T(8,128)(2,1)}, bf16[2,2,16,3584]{3,2,1,0:T(8,128)(2,1)S(1)}, u32[]{:S(2)}, u32[]{:S(2)}) collective-permute-start(bf16[2,2,16,3584]{3,2,1,0:T(8,128)(2,1)} %get-tuple-element.4.refs_0_), channel_id=1, source_target_pairs={{0,16},{16,32},{32,48},{48,0},{64,80},{80,96},{96,112},{112,64},{1... | collective-permute-start | bytes 1376264 | tf_op jit(solution)/shard_map/ppermute | solution.py:207
  78.3 0.7 collective-permute-start.7
  78.9 1.3 collective-permute-start.3
  80.2 7.4 %collective-permute-done.6.refs_8_ = bf16[2,2,16,3584]{3,2,1,0:T(8,128)(2,1)S(1)} collective-permute-done((bf16[2,2,16,3584]{3,2,1,0:T(8,128)(2,1)}, bf16[2,2,16,3584]{3,2,1,0:T(8,128)(2,1)S(1)}, u32[]{:S(2)}, u32[]{:S(2)}) %collective-permute-start.6) | collective-permute-done | bytes 458784 | tf_op jit(solution)/shard_map/ppermute | solution.py:208
  87.7 0.0 copy-start
  87.7 0.0 collective-permute-start.1
  87.7 0.9 collective-permute-done.2.refs_4_
  88.6 0.0 copy-start.1
  88.6 0.4 collective-permute-start.10
  88.9 0.0 collective-permute-done.refs_2_
  89.0 0.0 copy-start.2
  89.0 0.8 collective-permute-start.4
  89.7 7.7 %collective-permute-done.7.refs_9_ = bf16[2,2,16,3584]{3,2,1,0:T(8,128)(2,1)S(1)} collective-permute-done((bf16[2,2,16,3584]{3,2,1,0:T(8,128)(2,1)}, bf16[2,2,16,3584]{3,2,1,0:T(8,128)(2,1)S(1)}, u32[]{:S(2)}, u32[]{:S(2)}) %collective-permute-start.7) | collective-permute-done | bytes 458784 | tf_op jit(solution)/shard_map/ppermute | solution.py:206
  97.5 0.0 copy-start.3
  97.5 0.0 collective-permute-start.11
  97.5 0.9 collective-permute-done.3.refs_5_
  98.4 0.4 collective-permute-start.8
  98.8 0.0 collective-permute-done.1.refs_3_
  98.8 1.4 %collective-permute-start.9 = (bf16[2,2,16,3584]{3,2,1,0:T(8,128)(2,1)S(1)}, bf16[2,2,16,3584]{3,2,1,0:T(8,128)(2,1)}, u32[]{:S(2)}, u32[]{:S(2)}) collective-permute-start(bf16[2,2,16,3584]{3,2,1,0:T(8,128)(2,1)S(1)} %collective-permute-done.7.refs_9_), channel_id=1, source_target_pairs={{0,16},{16,32},{32,48},{48,0},{64,80},{80,96},{96,112},{112,64},{1... | collective-permute-start | bytes 1376264 | tf_op jit(solution)/shard_map/ppermute | solution.py:212
  100.1 7.3 %collective-permute-done.10.refs_12_ = bf16[2,2,16,3584]{3,2,1,0:T(8,128)(2,1)S(1)} collective-permute-done((bf16[2,2,16,3584]{3,2,1,0:T(8,128)(2,1)S(1)}, bf16[2,2,16,3584]{3,2,1,0:T(8,128)(2,1)S(1)}, u32[]{:S(2)}, u32[]{:S(2)}) %collective-permute-start.10) | collective-permute-done | bytes 458784 | tf_op jit(solution)/shard_map/ppermute | solution.py:213
  107.4 0.0 collective-permute-start.5
  107.4 1.1 collective-permute-done.4.refs_6_
  108.5 1.9 %collective-permute-start.12 = (bf16[2,2,16,3584]{3,2,1,0:T(8,128)(2,1)}, bf16[2,2,16,3584]{3,2,1,0:T(8,128)(2,1)}, u32[]{:S(2)}, u32[]{:S(2)}) collective-permute-start(bf16[2,2,16,3584]{3,2,1,0:T(8,128)(2,1)} %collective-permute-done.4.refs_6_), channel_id=1, source_target_pairs={{0,64},{16,80},{32,96},{48,112},{64,0},{80,16},{96,32},{112,48},{1... | collective-permute-start | bytes 1376264 | tf_op jit(solution)/shard_map/ppermute | solution.py:216
  110.4 0.0 collective-permute-done.11.refs_13_
  110.4 0.8 collective-permute-start.13
  111.3 0.1 broadcast_add_fusion.1
  111.4 0.6 pad_add_fusion.1.bands_ref
  111.9 2.5 %scales.1 = bf16[2,2,1,56]{3,2,1,0:T(2,128)(2,1)} custom-call(s32[1792]{0:T(1024)} %place_ref.3, s32[2]{0:T(128)} %refresh_ref.3, s32[1]{0:T(128)} %bitcast.4.rank_ref, bf16[8,16,120,128]{3,2,1,0:T(8,128)(2,1)} %bitcast.9.recv_ref), custom_call_target="tpu_custom_call" | custom-call | tf_op jit(solution)/shard_map/scales/pallas_call | solution.py:147
  114.5 1.2 copy.11
  115.7 1.5 %collective-permute-done.8.refs_10_ = bf16[2,2,16,3584]{3,2,1,0:T(8,128)(2,1)} collective-permute-done((bf16[2,2,16,3584]{3,2,1,0:T(8,128)(2,1)S(1)}, bf16[2,2,16,3584]{3,2,1,0:T(8,128)(2,1)}, u32[]{:S(2)}, u32[]{:S(2)}) %collective-permute-start.8) | collective-permute-done | bytes 458784 | tf_op jit(solution)/shard_map/ppermute | solution.py:211
  117.3 1.1 collective-permute-done.9.refs_11_
  118.4 9.8 %collective-permute-done.5.refs_7_ = bf16[2,2,16,3584]{3,2,1,0:T(8,128)(2,1)} collective-permute-done((bf16[2,2,16,3584]{3,2,1,0:T(8,128)(2,1)S(1)}, bf16[2,2,16,3584]{3,2,1,0:T(8,128)(2,1)}, u32[]{:S(2)}, u32[]{:S(2)}) %collective-permute-start.5) | collective-permute-done | bytes 458784 | tf_op jit(solution)/shard_map/ppermute | solution.py:214
  128.2 0.0 collective-permute-done.12.refs_14_
  128.2 0.0 collective-permute-done.13.refs_15_
  128.2 0.0 copy-done
  128.2 0.0 copy-done.1
  128.2 0.0 copy-done.2
  128.2 0.0 copy-done.3
  128.2 0.0 copy-done.4
  128.2 0.0 copy-done.5
  128.2 0.0 copy-done.6
  128.3 6.6 %join.1 = bf16[2,2,128,7168]{3,2,1,0:T(8,128)(2,1)} custom-call(s32[8]{0:T(128)} %pad_add_fusion.1.bands_ref, bf16[2,2,16,3584]{3,2,1,0:T(8,128)(2,1)} %get-tuple-element.4.refs_0_, bf16[2,2,16,3584]{3,2,1,0:T(8,128)(2,1)} %get-tuple-element.5.refs_1_, bf16[2,2,16,3584]{3,2,1,0:T(8,128)(2,1)} %copy-done.2, bf16[2,2,16,3584]{3,2,1,0:T(8,128)(2,1)} %copy-done.5, ...), custom_call_target="tpu_custom_call" | custom-call | tf_op jit(solution)/shard_map/join/pallas_call | solution.py:180
  (4 shorter events, 0.0 us)
Async XLA Ops:
  10.6 61.7 %all-to-all-start = ((bf16[128,120,128]{2,1,0:T(8,128)(2,1)}), bf16[128,120,128]{2,1,0:T(8,128)(2,1)}, u32[]{:S(2)}, u32[]{:S(2)}) async-start(bf16[128,120,128]{2,1,0:T(8,128)(2,1)} %bitcast.16), calls=%async_computation | async-start | bytes 7864320 | tf_op jit(solution)/shard_map/all_to_all | solution.py:224
  75.9 11.7 %collective-permute-start.6 = (bf16[2,2,16,3584]{3,2,1,0:T(8,128)(2,1)}, bf16[2,2,16,3584]{3,2,1,0:T(8,128)(2,1)S(1)}, u32[]{:S(2)}, u32[]{:S(2)}) collective-permute-start(bf16[2,2,16,3584]{3,2,1,0:T(8,128)(2,1)} %get-tuple-element.4.refs_0_), channel_id=1, source_target_pairs={{0,64},{16,80},{32,96},{48,112},{64,0},{80,16},{96,32},{112,48},{1... | collective-permute-start | bytes 1376264 | tf_op jit(solution)/shard_map/ppermute | solution.py:208
  76.8 11.7 %collective-permute-start.2 = (bf16[2,2,16,3584]{3,2,1,0:T(8,128)(2,1)}, bf16[2,2,16,3584]{3,2,1,0:T(8,128)(2,1)S(1)}, u32[]{:S(2)}, u32[]{:S(2)}) collective-permute-start(bf16[2,2,16,3584]{3,2,1,0:T(8,128)(2,1)} %get-tuple-element.4.refs_0_), channel_id=1, source_target_pairs={{0,48},{16,0},{32,16},{48,32},{64,112},{80,64},{96,80},{112,96},{1... | collective-permute-start | bytes 1376264 | tf_op jit(solution)/shard_map/ppermute | solution.py:207
  76.8 12.2 %collective-permute-start = (bf16[2,2,16,3584]{3,2,1,0:T(8,128)(2,1)}, bf16[2,2,16,3584]{3,2,1,0:T(8,128)(2,1)S(1)}, u32[]{:S(2)}, u32[]{:S(2)}) collective-permute-start(bf16[2,2,16,3584]{3,2,1,0:T(8,128)(2,1)} %get-tuple-element.4.refs_0_), channel_id=1, source_target_pairs={{0,16},{16,32},{32,48},{48,0},{64,80},{80,96},{96,112},{112,64},{1... | collective-permute-start | bytes 1376264 | tf_op jit(solution)/shard_map/ppermute | solution.py:207
  78.3 19.2 %collective-permute-start.7 = (bf16[2,2,16,3584]{3,2,1,0:T(8,128)(2,1)}, bf16[2,2,16,3584]{3,2,1,0:T(8,128)(2,1)S(1)}, u32[]{:S(2)}, u32[]{:S(2)}) collective-permute-start(bf16[2,2,16,3584]{3,2,1,0:T(8,128)(2,1)} %get-tuple-element.5.refs_1_), channel_id=1, source_target_pairs={{0,64},{16,80},{32,96},{48,112},{64,0},{80,16},{96,32},{112,48},{1... | collective-permute-start | bytes 1376264 | tf_op jit(solution)/shard_map/ppermute | solution.py:206
  78.9 19.5 %collective-permute-start.3 = (bf16[2,2,16,3584]{3,2,1,0:T(8,128)(2,1)}, bf16[2,2,16,3584]{3,2,1,0:T(8,128)(2,1)S(1)}, u32[]{:S(2)}, u32[]{:S(2)}) collective-permute-start(bf16[2,2,16,3584]{3,2,1,0:T(8,128)(2,1)} %get-tuple-element.5.refs_1_), channel_id=1, source_target_pairs={{0,48},{16,0},{32,16},{48,32},{64,112},{80,64},{96,80},{112,96},{1... | collective-permute-start | bytes 1376264 | tf_op jit(solution)/shard_map/ppermute | solution.py:210
  87.7 40.5 %copy-start = (bf16[2,2,16,3584]{3,2,1,0:T(8,128)(2,1)}, bf16[2,2,16,3584]{3,2,1,0:T(8,128)(2,1)S(1)}, u32[]{:S(2)}) copy-start(bf16[2,2,16,3584]{3,2,1,0:T(8,128)(2,1)S(1)} %collective-permute-done.6.refs_8_) | copy-start | bytes 1376260
  87.7 11.1 %collective-permute-start.1 = (bf16[2,2,16,3584]{3,2,1,0:T(8,128)(2,1)}, bf16[2,2,16,3584]{3,2,1,0:T(8,128)(2,1)S(1)}, u32[]{:S(2)}, u32[]{:S(2)}) collective-permute-start(bf16[2,2,16,3584]{3,2,1,0:T(8,128)(2,1)} %get-tuple-element.5.refs_1_), channel_id=1, source_target_pairs={{0,16},{16,32},{32,48},{48,0},{64,80},{80,96},{96,112},{112,64},{1... | collective-permute-start | bytes 1376264 | tf_op jit(solution)/shard_map/ppermute | solution.py:210
  88.6 39.6 %copy-start.1 = (bf16[2,2,16,3584]{3,2,1,0:T(8,128)(2,1)}, bf16[2,2,16,3584]{3,2,1,0:T(8,128)(2,1)S(1)}, u32[]{:S(2)}) copy-start(bf16[2,2,16,3584]{3,2,1,0:T(8,128)(2,1)S(1)} %collective-permute-done.2.refs_4_) | copy-start | bytes 1376260
  88.6 18.9 %collective-permute-start.10 = (bf16[2,2,16,3584]{3,2,1,0:T(8,128)(2,1)S(1)}, bf16[2,2,16,3584]{3,2,1,0:T(8,128)(2,1)S(1)}, u32[]{:S(2)}, u32[]{:S(2)}) collective-permute-start(bf16[2,2,16,3584]{3,2,1,0:T(8,128)(2,1)S(1)} %collective-permute-done.2.refs_4_), channel_id=1, source_target_pairs={{0,64},{16,80},{32,96},{48,112},{64,0},{80,16},{96,32},{112,48},{1... | collective-permute-start | bytes 1376264 | tf_op jit(solution)/shard_map/ppermute | solution.py:213
  89.0 39.2 %copy-start.2 = (bf16[2,2,16,3584]{3,2,1,0:T(8,128)(2,1)}, bf16[2,2,16,3584]{3,2,1,0:T(8,128)(2,1)S(1)}, u32[]{:S(2)}) copy-start(bf16[2,2,16,3584]{3,2,1,0:T(8,128)(2,1)S(1)} %collective-permute-done.refs_2_) | copy-start | bytes 1376260
  89.0 19.6 %collective-permute-start.4 = (bf16[2,2,16,3584]{3,2,1,0:T(8,128)(2,1)S(1)}, bf16[2,2,16,3584]{3,2,1,0:T(8,128)(2,1)}, u32[]{:S(2)}, u32[]{:S(2)}) collective-permute-start(bf16[2,2,16,3584]{3,2,1,0:T(8,128)(2,1)S(1)} %collective-permute-done.refs_2_), channel_id=1, source_target_pairs={{0,16},{16,32},{32,48},{48,0},{64,80},{80,96},{96,112},{112,64},{1... | collective-permute-start | bytes 1376264 | tf_op jit(solution)/shard_map/ppermute | solution.py:209
  97.5 30.7 %copy-start.3 = (bf16[2,2,16,3584]{3,2,1,0:T(8,128)(2,1)}, bf16[2,2,16,3584]{3,2,1,0:T(8,128)(2,1)S(1)}, u32[]{:S(2)}) copy-start(bf16[2,2,16,3584]{3,2,1,0:T(8,128)(2,1)S(1)} %collective-permute-done.7.refs_9_) | copy-start | bytes 1376260
  97.5 12.9 %collective-permute-start.11 = (bf16[2,2,16,3584]{3,2,1,0:T(8,128)(2,1)S(1)}, bf16[2,2,16,3584]{3,2,1,0:T(8,128)(2,1)}, u32[]{:S(2)}, u32[]{:S(2)}) collective-permute-start(bf16[2,2,16,3584]{3,2,1,0:T(8,128)(2,1)S(1)} %collective-permute-done.7.refs_9_), channel_id=1, source_target_pairs={{0,48},{16,0},{32,16},{48,32},{64,112},{80,64},{96,80},{112,96},{1... | collective-permute-start | bytes 1376264 | tf_op jit(solution)/shard_map/ppermute | solution.py:212
  98.4 29.8 %copy-start.4 = (bf16[2,2,16,3584]{3,2,1,0:T(8,128)(2,1)}, bf16[2,2,16,3584]{3,2,1,0:T(8,128)(2,1)S(1)}, u32[]{:S(2)}) copy-start(bf16[2,2,16,3584]{3,2,1,0:T(8,128)(2,1)S(1)} %collective-permute-done.3.refs_5_) | copy-start | bytes 1376260
  98.4 18.9 %collective-permute-start.8 = (bf16[2,2,16,3584]{3,2,1,0:T(8,128)(2,1)S(1)}, bf16[2,2,16,3584]{3,2,1,0:T(8,128)(2,1)}, u32[]{:S(2)}, u32[]{:S(2)}) collective-permute-start(bf16[2,2,16,3584]{3,2,1,0:T(8,128)(2,1)S(1)} %collective-permute-done.refs_2_), channel_id=1, source_target_pairs={{0,64},{16,80},{32,96},{48,112},{64,0},{80,16},{96,32},{112,48},{1... | collective-permute-start | bytes 1376264 | tf_op jit(solution)/shard_map/ppermute | solution.py:211
  98.8 29.5 %copy-start.5 = (bf16[2,2,16,3584]{3,2,1,0:T(8,128)(2,1)}, bf16[2,2,16,3584]{3,2,1,0:T(8,128)(2,1)S(1)}, u32[]{:S(2)}) copy-start(bf16[2,2,16,3584]{3,2,1,0:T(8,128)(2,1)S(1)} %collective-permute-done.1.refs_3_) | copy-start | bytes 1376260
  98.8 19.6 %collective-permute-start.9 = (bf16[2,2,16,3584]{3,2,1,0:T(8,128)(2,1)S(1)}, bf16[2,2,16,3584]{3,2,1,0:T(8,128)(2,1)}, u32[]{:S(2)}, u32[]{:S(2)}) collective-permute-start(bf16[2,2,16,3584]{3,2,1,0:T(8,128)(2,1)S(1)} %collective-permute-done.7.refs_9_), channel_id=1, source_target_pairs={{0,16},{16,32},{32,48},{48,0},{64,80},{80,96},{96,112},{112,64},{1... | collective-permute-start | bytes 1376264 | tf_op jit(solution)/shard_map/ppermute | solution.py:212
  107.4 20.8 %copy-start.6 = (bf16[2,2,16,3584]{3,2,1,0:T(8,128)(2,1)}, bf16[2,2,16,3584]{3,2,1,0:T(8,128)(2,1)S(1)}, u32[]{:S(2)}) copy-start(bf16[2,2,16,3584]{3,2,1,0:T(8,128)(2,1)S(1)} %collective-permute-done.10.refs_12_) | copy-start | bytes 1376260
  107.4 20.8 %collective-permute-start.5 = (bf16[2,2,16,3584]{3,2,1,0:T(8,128)(2,1)S(1)}, bf16[2,2,16,3584]{3,2,1,0:T(8,128)(2,1)}, u32[]{:S(2)}, u32[]{:S(2)}) collective-permute-start(bf16[2,2,16,3584]{3,2,1,0:T(8,128)(2,1)S(1)} %collective-permute-done.1.refs_3_), channel_id=1, source_target_pairs={{0,16},{16,32},{32,48},{48,0},{64,80},{80,96},{96,112},{112,64},{1... | collective-permute-start | bytes 1376264 | tf_op jit(solution)/shard_map/ppermute | solution.py:214
  108.5 19.7 %collective-permute-start.12 = (bf16[2,2,16,3584]{3,2,1,0:T(8,128)(2,1)}, bf16[2,2,16,3584]{3,2,1,0:T(8,128)(2,1)}, u32[]{:S(2)}, u32[]{:S(2)}) collective-permute-start(bf16[2,2,16,3584]{3,2,1,0:T(8,128)(2,1)} %collective-permute-done.4.refs_6_), channel_id=1, source_target_pairs={{0,64},{16,80},{32,96},{48,112},{64,0},{80,16},{96,32},{112,48},{1... | collective-permute-start | bytes 1376264 | tf_op jit(solution)/shard_map/ppermute | solution.py:216
  110.4 17.8 %collective-permute-start.13 = (bf16[2,2,16,3584]{3,2,1,0:T(8,128)(2,1)}, bf16[2,2,16,3584]{3,2,1,0:T(8,128)(2,1)}, u32[]{:S(2)}, u32[]{:S(2)}) collective-permute-start(bf16[2,2,16,3584]{3,2,1,0:T(8,128)(2,1)} %collective-permute-done.11.refs_13_), channel_id=1, source_target_pairs={{0,48},{16,0},{32,16},{48,32},{64,112},{80,64},{96,80},{112,96},{1... | collective-permute-start | bytes 1376264 | tf_op jit(solution)/shard_map/ppermute | solution.py:215
